TPU v7x, 32 devices: a whole 2x2x4 slice. The times are simulated.
32 devices in a mesh: ulysses: 4 (over z), blk: 2 (over y), tensor: 4 (over x, core).
Axes of the slice: x: 2, y: 2, z: 4, core: 2. Of those that a mesh axis runs over, the one named last changes fastest.
Arguments:
- tokens: bfloat16 [2048, 5120], P(('ulysses', 'blk'), 'tensor'), may hold values from -20 to 20
- w_qkv: bfloat16 [5120, 3, 4096], P(None, None, ('ulysses', 'tensor')), may hold values from -2 to 2
- qkv_scale: float32 [3, 32], P(None, ('ulysses', 'tensor')), may hold values from 0.6 to 9
- block_mask: int32 [32, 16, 16], P(('ulysses', 'tensor')), may hold values from 0 to 1, as said below
- w_out: bfloat16 [4, 1024, 5120], P(None, 'tensor'), may hold values from -0.125 to 0.125
Outputs:
- mixed: bfloat16 [2048, 5120], P(('ulysses', 'blk'), 'tensor')
Inputs may be any that keep to these rules, and one draw needn't show every extreme that they name: `block_mask`: 0 or 1; the share of ones differs from head to head.
All inputs are finite; a program needn't handle non-finite values.
Results may differ from a plain program's by a relative error of at most 0.015.
Values may be sent and summed in bfloat16 or wider, within the bound.
A program may use at most 128 MiB of HBM per device.

v0:
```python
import math

import jax
import jax.numpy as jnp
from jax import lax
from jax.sharding import PartitionSpec as P


def local(tokens, w_qkv, qkv_scale, block_mask, w_out):
    group_count = lax.axis_size("ulysses")
    tensor_count = lax.axis_size("tensor")
    cycle_count = lax.axis_size("blk")
    tok_rows, feat_cols = tokens.shape
    width_all, triple, head_cols = w_qkv.shape
    heads_here = qkv_scale.shape[1]
    head_dim = head_cols // heads_here
    blocks_all = block_mask.shape[1]
    group_rows = tok_rows * group_count
    block_rows = cycle_count * group_rows // blocks_all
    start_sum = jnp.zeros((group_count, tok_rows, triple, head_cols), jnp.float32)
    pieces = lax.all_gather(tokens[None], ("ulysses", "tensor"), axis=0, tiled=True)

    def one_shard(which, accum):
        group_id = which // tensor_count
        feature_id = which % tensor_count
        weights = lax.dynamic_slice_in_dim(w_qkv, feature_id * feat_cols, feat_cols, 0)
        token_part = lax.dynamic_index_in_dim(pieces, which, 0, keepdims=False)
        product = jnp.einsum("rd,dcn->rcn", token_part, weights, preferred_element_type=jnp.float32)
        current = lax.dynamic_index_in_dim(accum, group_id, 0, keepdims=False)
        return lax.dynamic_update_index_in_dim(accum, current + product, group_id, 0)

    projected = lax.fori_loop(0, pieces.shape[0], one_shard, start_sum)
    projected = (
        projected.reshape(group_rows, triple, heads_here, head_dim) * qkv_scale[None, :, :, None]
    )
    projected = projected.astype(jnp.bfloat16)
    queries = projected[:, 0]
    keys = projected[:, 1]
    values = projected[:, 2]
    cycle_index = lax.axis_index("blk")
    local_rows = jnp.arange(group_rows, dtype=jnp.int32)
    query_pos = (
        local_rows // tok_rows * cycle_count + cycle_index
    ) * tok_rows + local_rows % tok_rows
    query_block = query_pos // block_rows
    block_ids = jnp.arange(blocks_all, dtype=jnp.int32)
    query_onehot = (query_block[:, None] == block_ids[None, :]).astype(jnp.bfloat16)
    query_live = jnp.einsum(
        "qn,hnm->hqm",
        query_onehot,
        block_mask.astype(jnp.bfloat16),
        preferred_element_type=jnp.float32,
    ).astype(jnp.bfloat16)
    score_scale = 1.0 / math.sqrt(head_dim)
    start_state = (
        jnp.full((heads_here, group_rows), -1e30, jnp.float32),
        jnp.zeros((heads_here, group_rows), jnp.float32),
        jnp.zeros((heads_here, group_rows, head_dim), jnp.float32),
    )
    key_all = lax.all_gather(keys, "blk", axis=0, tiled=True)
    value_all = lax.all_gather(values, "blk", axis=0, tiled=True)

    def one_block(which, state):
        highest, denominator, numerator = state
        key_part = lax.dynamic_slice_in_dim(key_all, which * group_rows, group_rows, 0)
        value_part = lax.dynamic_slice_in_dim(value_all, which * group_rows, group_rows, 0)
        gathered_row = which * group_rows + local_rows
        owner_cycle = gathered_row // group_rows
        inner_row = gathered_row % group_rows
        key_pos = (
            inner_row // tok_rows * cycle_count + owner_cycle
        ) * tok_rows + inner_row % tok_rows
        key_block = key_pos // block_rows
        key_onehot = (key_block[:, None] == block_ids[None, :]).astype(jnp.bfloat16)
        allowed = (
            jnp.einsum("hqn,kn->hqk", query_live, key_onehot, preferred_element_type=jnp.float32)
            > 0.5
        )
        allowed = allowed | (query_block[:, None] == key_block[None, :])[None]
        scores = (
            jnp.einsum("qhd,khd->hqk", queries, key_part, preferred_element_type=jnp.float32)
            * score_scale
        )
        scores = jnp.where(allowed, scores, -jnp.inf)
        new_high = jnp.maximum(highest, jnp.max(scores, axis=-1))
        weights = jnp.exp(scores - new_high[..., None])
        factor = jnp.exp(highest - new_high)
        denominator = denominator * factor + jnp.sum(weights, axis=-1)
        numerator = numerator * factor[..., None] + jnp.einsum(
            "hqk,khd->hqd",
            weights.astype(jnp.bfloat16),
            value_part,
            preferred_element_type=jnp.float32,
        )
        return (new_high, denominator, numerator)

    highest, denominator, numerator = lax.fori_loop(
        0, key_all.shape[0] // group_rows, one_block, start_state
    )
    attended = (numerator / denominator[..., None]).astype(jnp.bfloat16)
    grouped = attended.reshape(heads_here, group_count, tok_rows, head_dim)
    arrived = lax.all_to_all(grouped, "ulysses", split_axis=1, concat_axis=0, tiled=True)
    out_rows = w_out.reshape(group_count * heads_here, head_dim, w_out.shape[2])
    partial_value = jnp.einsum(
        "grd,gdf->rf", arrived[:, 0], out_rows, preferred_element_type=jnp.float32
    )
    summed = lax.psum_scatter(
        partial_value.astype(jnp.bfloat16), "tensor", scatter_dimension=1, tiled=True
    )
    return summed


def solution(mesh):
    return jax.shard_map(
        local,
        mesh=mesh,
        in_specs=(
            P(("ulysses", "blk"), "tensor"),
            P(None, None, ("ulysses", "tensor")),
            P(None, ("ulysses", "tensor")),
            P(("ulysses", "tensor"), None, None),
            P(None, "tensor", None),
        ),
        out_specs=P(("ulysses", "blk"), "tensor"),
        check_vma=False,
    )
```

profile of v0, /device:TPU:0, one launch (start us, length us, event | category | flops | bytes accessed | tf_op | source)
XLA Modules:
  0.0 308.4 jit_solution(13720380740776168870)
XLA Ops:
  6.5 0.7 all-gather.7.cloned.1.call-update
  7.3 0.8 copy.21
  8.1 91.8 %all-gather.7.cloned.1.call-done = bf16[4096,1280]{1,0:T(8,128)(2,1)} async-done(((bf16[256,1280]{1,0:T(8,128)(2,1)}), bf16[4096,1280]{1,0:T(8,128)(2,1)}) %all-gather.7.cloned.1.call-update) | async-done | bytes 10485776 | tf_op jit(solution)/shard_map/all_gather | solution.py:21
  99.9 0.3 broadcast_in_dim.66.clone
  100.1 57.4 %while.36 = (s32[]{:T(128)}, f32[4,256,3,256]{3,1,0,2:T(8,128)S(1)}, bf16[16,256,1280]{2,1,0:T(8,128)(2,1)}, bf16[5120,3,256]{2,0,1:T(8,128)(2,1)}, s32[]{:T(128...) while((s32[]{:T(128)}, ...), condition=%wide.region_1.2_spmd, body=%wide.region_0.1_spmd.sunk | while | flops 503513120 | bytes 5768004 | solution.py:32
  100.2 0.9 constant_dynamic-slice_fusion.5
  101.1 2.6 fusion.106
  103.8 0.9 constant_dynamic-slice_fusion.5
  104.7 2.6 fusion.106
  107.3 0.9 constant_dynamic-slice_fusion.5
  108.3 2.6 fusion.106
  110.9 0.9 constant_dynamic-slice_fusion.5
  111.9 2.6 fusion.106
  114.5 0.9 constant_dynamic-slice_fusion.5
  115.5 2.6 fusion.106
  118.1 0.9 constant_dynamic-slice_fusion.5
  119.1 2.6 fusion.106
  121.7 0.9 constant_dynamic-slice_fusion.5
  122.6 2.6 fusion.106
  125.3 0.9 constant_dynamic-slice_fusion.5
  126.2 2.6 fusion.106
  128.9 0.9 constant_dynamic-slice_fusion.5
  129.8 2.6 fusion.106
  132.5 0.9 constant_dynamic-slice_fusion.5
  133.4 2.6 fusion.106
  136.0 0.9 constant_dynamic-slice_fusion.5
  137.0 2.6 fusion.106
  139.6 0.9 constant_dynamic-slice_fusion.5
  140.6 2.6 fusion.106
  143.2 0.9 constant_dynamic-slice_fusion.5
  144.2 2.6 fusion.106
  146.8 0.9 constant_dynamic-slice_fusion.5
  147.8 2.6 fusion.106
  150.4 0.9 constant_dynamic-slice_fusion.5
  151.3 2.6 fusion.106
  154.0 0.9 constant_dynamic-slice_fusion.5
  154.9 2.6 fusion.106
  157.6 3.0 reshape.217
  160.6 3.0 multiply_convert_fusion
  163.6 2.1 slice_bitcast_fusion
  165.8 0.7 all-gather.11.cloned.1.call-update
  166.6 0.1 copy.19
  166.7 0.2 fusion.69
  166.9 18.5 %all-gather.9.cloned.1.call-done = bf16[2048,1,2,128]{3,2,1,0:T(2,128)(2,1)} async-done(((bf16[1024,1,2,128]{3,2,1,0:T(2,128)(2,1)}), bf16[2048,1,2,128]{3,2,1,0:T(2,128)(2,1)}) %all-gather.9.cloned.1.call-update) | async-done | bytes 1048592 | tf_op jit(solution)/shard_map/all_gather | solution.py:60
  185.4 22.9 %all-gather.11.cloned.1.call-done = bf16[2048,1,2,128]{3,2,1,0:T(2,128)(2,1)} async-done(((bf16[1024,1,2,128]{3,2,1,0:T(2,128)(2,1)}), bf16[2048,1,2,128]{3,2,1,0:T(2,128)(2,1)}) %all-gather.11.cloned.1.call-update) | async-done | bytes 1048592 | tf_op jit(solution)/shard_map/all_gather | solution.py:61
  208.3 33.7 %while.37 = (s32[]{:T(128)}, f32[2,1024]{1,0:T(2,128)S(1)}, f32[2,1024]{1,0:T(2,128)S(1)}, f32[2,1024,128]{2,1,0:T(8,128)S(1)}, bf16[2,1024,16]{1,2,0:T(8,128)(2...) while((s32[]{:T(128)}, f32[2,1024]{1,0:T(2,128)S(1)}, ...), condition=%wide.region_5.6_spmd.clone, body=%wide.region_2.5_spmd.clone.sunk | while | flops 1161677824 | bytes 83579104 | solution.py:97
  208.3 1.9 constant_dynamic-slice_fusion.6
  210.2 0.7 broadcast_compare_fusion.2
  210.9 1.3 fusion.112
  212.2 4.8 %fusion.113 = (f32[2,1024]{1,0:T(2,128)S(1)}, f32[2,1024,1024]{1,2,0:T(8,128)}) fusion(bf16[1024,2,128]{2,0,1:T(8,128)(2,1)S(1)} %get-tuple-element.690, bf16[1024,2,128]{2,1,0:T(2,128)(2,1)S(1)} %get-tuple-element.614, pred[1024,1024]{0,1:T(8,128)(4,1)S(1)} %broadcast_compare_fusion.2, f32[1024,2,1024]{2,0,1:T(8,128)S(1)} %fusion.112), kind=kOutput, calls=%fused_computation.126.clone.1 | convolution fusion | flops 547354624 | bytes 18882560 | tf_op jit(solution)/shard_map/while/body/eval_jaxpr/qhd,khd->hqk/dot_general | solution.py:81
  217.0 4.7 %fusion.115 = f32[2,1024]{1,0:T(2,128)S(1)} fusion(f32[2,1024,1024]{1,2,0:T(8,128)} %get-tuple-element.618, f32[2,1024]{1,0:T(2,128)S(1)} %fusion.114), kind=kLoop, calls=%fused_computation.16.clone.1 | loop fusion | flops 4192256 | bytes 8404992 | tf_op jit(solution)/shard_map/while/body/eval_jaxpr/reduce_sum | solution.py:88
  221.7 1.0 copy-done
  222.7 2.3 fusion.117
  225.1 1.9 constant_dynamic-slice_fusion.6
  227.1 0.7 broadcast_compare_fusion.2
  227.7 1.3 fusion.112
  229.0 4.8 %fusion.113 = (f32[2,1024]{1,0:T(2,128)S(1)}, f32[2,1024,1024]{1,2,0:T(8,128)}) fusion(bf16[1024,2,128]{2,0,1:T(8,128)(2,1)S(1)} %get-tuple-element.690, bf16[1024,2,128]{2,1,0:T(2,128)(2,1)S(1)} %get-tuple-element.614, pred[1024,1024]{0,1:T(8,128)(4,1)S(1)} %broadcast_compare_fusion.2, f32[1024,2,1024]{2,0,1:T(8,128)S(1)} %fusion.112), kind=kOutput, calls=%fused_computation.126.clone.1 | convolution fusion | flops 547354624 | bytes 18882560 | tf_op jit(solution)/shard_map/while/body/eval_jaxpr/qhd,khd->hqk/dot_general | solution.py:81
  233.8 4.7 %fusion.115 = f32[2,1024]{1,0:T(2,128)S(1)} fusion(f32[2,1024,1024]{1,2,0:T(8,128)} %get-tuple-element.618, f32[2,1024]{1,0:T(2,128)S(1)} %fusion.114), kind=kLoop, calls=%fused_computation.16.clone.1 | loop fusion | flops 4192256 | bytes 8404992 | tf_op jit(solution)/shard_map/while/body/eval_jaxpr/reduce_sum | solution.py:88
  238.6 1.0 copy-done
  239.6 2.3 fusion.117
  242.0 0.3 divide_convert_fusion
  242.3 18.7 %all_to_all.15 = bf16[2,4,256,128]{3,2,0,1:T(8,128)(2,1)S(1)} all-to-all(bf16[2,4,256,128]{3,2,0,1:T(8,128)(2,1)S(1)} %copy.27), channel_id=1, replica_groups=mesh['ulysses'=4,'blk'=2,'tensor'=4] {'ulysses'}, dimensions={1} | all-to-all | bytes 1048576 | tf_op jit(solution)/shard_map/all_to_all | solution.py:102
  261.1 8.1 %fusion.68 = bf16[256,5120]{1,0:T(8,128)(2,1)} fusion(bf16[8,256,128]{2,1,0:T(8,128)(2,1)S(1)} %bitcast.73, bf16[8,128,5120]{2,1,0:T(8,128)(2,1)} %bitcast.76), kind=kOutput, calls=%fused_computation.94 | convolution fusion | flops 2685665280 | bytes 13631488 | tf_op jit(solution)/shard_map/grd,gdf->rf/dot_general | solution.py:104
  269.2 32.7 %reduce-scatter.2.cloned.1.call-done = bf16[256,1280]{1,0:T(8,128)(2,1)} async-done(((bf16[256,5120]{1,0:T(8,128)(2,1)}), bf16[256,1280]{1,0:T(8,128)(2,1)}) %reduce-scatter.2.cloned.1.call-update) | async-done | bytes 655376 | tf_op jit(solution)/shard_map/reduce_scatter | solution.py:107
  (26 shorter events, 0.4 us)
Async XLA Ops:
  6.5 93.3 %all-gather.7.cloned.1.call-start = ((), (), s32[]{:S(2)}) async-start(), calls=%async_computation.3 | async-start | bytes 11141120 | tf_op jit(solution)/shard_map/all_gather | solution.py:21
  7.3 178.2 %all-gather.9.cloned.1.call-start = ((), (), s32[]{:S(2)}) async-start(), calls=%async_computation.4 | async-start | bytes 1572864 | tf_op jit(solution)/shard_map/all_gather | solution.py:60
  157.5 9.0 %copy-start.1 = (s32[2,16,16]{2,1,0:T(8,128)S(1)}, s32[2,16,16]{2,1,0:T(8,128)}, u32[]{:S(2)}) copy-start(s32[2,16,16]{2,1,0:T(8,128)} %param.12) | copy-start | bytes 6148
  165.7 42.6 %all-gather.11.cloned.1.call-start = ((), (), s32[]{:S(2)}) async-start(), calls=%async_computation.5 | async-start | bytes 1572864 | tf_op jit(solution)/shard_map/all_gather | solution.py:61
  166.5 135.4 %reduce-scatter.2.cloned.1.call-start = ((), (), s32[]{:S(2)}) async-start(), calls=%async_computation.2 | async-start | bytes 3276800 | tf_op jit(solution)/shard_map/reduce_scatter | solution.py:107
  217.0 5.8 %copy-start = (f32[2,1024,1024]{1,2,0:T(8,128)S(1)}, f32[2,1024,1024]{1,2,0:T(8,128)}, u32[]{:S(2)}) copy-start(f32[2,1024,1024]{1,2,0:T(8,128)} %get-tuple-element.618) | copy-start | bytes 25165828 | tf_op jit(solution)/shard_map/while
  233.8 5.8 %copy-start = (f32[2,1024,1024]{1,2,0:T(8,128)S(1)}, f32[2,1024,1024]{1,2,0:T(8,128)}, u32[]{:S(2)}) copy-start(f32[2,1024,1024]{1,2,0:T(8,128)} %get-tuple-element.618) | copy-start | bytes 25165828 | tf_op jit(solution)/shard_map/while
Sparse Core Ops, SparseCore 0:
  9.6 90.2 all-gather.6
  165.8 19.5 all-gather.8
  187.0 21.2 all-gather.10
  269.4 32.4 reduce-scatter.1
where the time goes:
time: 309 us; the launch traced here: 308 us
  waiting for transfers between devices  167 us (54%)
  matrix products  66.7 us (22%)
  local copies, waits for them, and re-layouts  27.4 us (9%)
  blocking collectives  18.7 us (6%)
  other arithmetic  14.2 us (5%)
  between operations  13.2 us (4%)
    all_gather x1, waiting for transfers between devices, local(): lax.all_gather(tokens[None], ('ulysses', 'tensor'), axis=0, tiled=True)  91.8 us
    dot_general x16, matrix products, one_shard(): jnp.einsum('rd,dcn->rcn', token_part, weights, preferred_element_type=jnp...  41.7 us
    reduce_scatter x1, waiting for transfers between devices, local(): lax.psum_scatter(partial_value.astype(jnp.bfloat16), 'tensor', scatter_di...  32.7 us
    all_gather x1, waiting for transfers between devices, local(): value_all = lax.all_gather(values, 'blk', axis=0, tiled=True)  22.9 us
    all_to_all x1, blocking collectives, local(): lax.all_to_all(grouped, 'ulysses', split_axis=1, concat_axis=0, tiled=True)  18.7 us
    all_gather x1, waiting for transfers between devices, local(): key_all = lax.all_gather(keys, 'blk', axis=0, tiled=True)  18.5 us
    dynamic_slice x16, local copies, waits for them, and re-layouts, one_shard(): current = lax.dynamic_index_in_dim(accum, group_id, 0, keepdims=False)  15.1 us
    dot_general x2, matrix products, one_block(): jnp.einsum('qhd,khd->hqk', queries, key_part, preferred_element_type=jnp....  9.53 us
  transfers between devices with their start and end apart: 4, of which 4 were waited for; matrix products, arithmetic and copies ran while one was open for 0% of the time, Pallas kernels for 0%

commit v1 on v0

v1 whole, which is shorter than its diff:
```python
import functools
import math

import jax
import jax.numpy as jnp
from jax import lax
from jax.experimental import pallas as pl
from jax.experimental.pallas import tpu as pltpu
from jax.sharding import PartitionSpec as P

SUB = 2
F32 = jnp.float32
BF16 = jnp.bfloat16


def kernel(U, B, T, x_ref, w_hbm, scale_ref, bias_ref, wo_hbm, out_ref,
           g, w, wo, q, kv, att, arr, part, got, mid, far_got,
           w_sem, wo_sem, own_sem,
           zs, zr, up_s, dn_s, xs, xr, cs, cr, fs, fr, ks, kr, as_, ar, ps, pr, ms, mr):
    z, y, t = lax.axis_index("ulysses"), lax.axis_index("blk"), lax.axis_index("tensor")
    near = t + 1 - 2 * lax.rem(t, 2)
    far = lax.rem(t + T // 2, T)
    cross = lax.rem(near + T // 2, T)
    rows, feats = x_ref.shape
    R = rows // SUB
    H, HD = q.shape[0], q.shape[2]
    N = U * SUB
    nbp = rows // bias_ref.shape[3]
    block = bias_ref.shape[3]

    w_copy = pltpu.make_async_copy(w_hbm, w, w_sem)
    w_copy.start()
    wo_copies = [
        pltpu.make_async_copy(wo_hbm.at[:, :, pl.ds(j * feats, feats)], wo.at[j], wo_sem.at[j])
        for j in range(T)
    ]
    for c in wo_copies:
        c.start()
    for s in range(SUB):
        c = pltpu.make_async_copy(x_ref.at[pl.ds(s * R, R)], g.at[z * SUB + s, t], own_sem.at[s])
        c.start()
    for s in range(SUB):
        pltpu.make_async_copy(x_ref.at[pl.ds(s * R, R)], g.at[z * SUB + s, t], own_sem.at[s]).wait()

    barrier = pltpu.get_barrier_semaphore()
    for d in range(1, U):
        pl.semaphore_signal(barrier, inc=1, device_id={"ulysses": lax.rem(z + d, U)})
    for d in range(1, B):
        pl.semaphore_signal(barrier, inc=1, device_id={"blk": lax.rem(y + d, B)})
    pl.semaphore_signal(barrier, inc=1, device_id={"tensor": near})
    pl.semaphore_signal(barrier, inc=1, device_id={"tensor": far})
    pl.semaphore_wait(barrier, (U - 1) + (B - 1) + 2)

    def order(p):
        m = jnp.minimum(z, U - 1 - z)
        half = (p + 1) // 2
        near_z = jnp.where(lax.rem(p, 2) == 1, z - half, z + half)
        far_z = jnp.where(z < U - 1 - z, p, U - 1 - p)
        return jnp.where(p <= 2 * m, near_z, far_z)

    def remote(src, dst, send, recv, **where):
        return pltpu.make_async_remote_copy(
            src_ref=src, dst_ref=dst, send_sem=send, recv_sem=recv, device_id=where
        )

    def piece_of(i):
        zz = order(i // SUB)
        return zz, zz * SUB + lax.rem(i, SUB)

    def z_copy(slot, send, target):
        return remote(g.at[slot, t], g.at[slot, t], send, zr.at[slot], ulysses=target)

    def x_copy(slot, col, i):
        return remote(g.at[slot, col], g.at[slot, col], xs.at[i], xr.at[i], tensor=far)

    def c_copy(slot, col, i):
        return remote(g.at[slot, col], g.at[slot, col], cs.at[i], cr.at[i], tensor=near)

    def f_copy(slot, col, i):
        return remote(g.at[slot, col], g.at[slot, col], fs.at[i], fr.at[i], tensor=near)

    def kv_copy(who, slot, i, d):
        view = kv.at[who, :, :, pl.ds(pl.multiple_of(slot * R, R), R), :]
        return remote(view, view, ks.at[d - 1, i], kr.at[who, i], blk=lax.rem(y + d, B))

    def forward(i, act):
        zz, slot = piece_of(i)
        own = i < SUB
        s = lax.rem(i, SUB)

        @pl.when(own & (z + 1 < U))
        def _():
            act(z_copy(slot, up_s.at[s], z + 1))

        @pl.when(own & (z > 0))
        def _():
            act(z_copy(slot, dn_s.at[s], z - 1))

        nxt = jnp.where(zz < z, z + 1, z - 1)

        @pl.when(jnp.logical_not(own) & (nxt >= 0) & (nxt < U))
        def _():
            act(z_copy(slot, zs.at[slot], nxt))

    def step(j, carry):
        @pl.when(j < N)
        def _():
            zz, slot = piece_of(j)

            @pl.when(j >= SUB)
            def _():
                z_copy(slot, zs.at[slot], lax.rem(z + 1, U)).wait_recv()

            forward(j, lambda c: c.start())
            x_copy(slot, t, j).start()
            c_copy(slot, t, j).start()

        @pl.when(j >= SUB)
        def _():
            i = j - SUB
            zz, slot = piece_of(i)
            x_copy(slot, far, i).wait_recv()
            f_copy(slot, far, i).start()
            c_copy(slot, near, i).wait_recv()

            @pl.when(i == 0)
            def _():
                w_copy.wait()

            f_copy(slot, cross, i).wait_recv()
            for c in range(3):
                acc = jnp.zeros((R, H * HD), F32)
                for k in range(T):
                    acc += jnp.dot(
                        g[slot, k], w[c, pl.ds(k * feats, feats), :], preferred_element_type=F32
                    )
                for h in range(H):
                    val = (acc[:, h * HD:(h + 1) * HD] * scale_ref[c, h]).astype(BF16)
                    at = pl.ds(pl.multiple_of(slot * R, R), R)
                    if c == 0:
                        q[h, at, :] = val
                    else:
                        kv[y, c - 1, h, at, :] = val
            for d in range(1, B):
                kv_copy(y, slot, i, d).start()

        return carry

    lax.fori_loop(0, N + SUB, step, 0)

    def kv_wait(i, carry):
        zz, slot = piece_of(i)
        for d in range(1, B):
            kv_copy(lax.rem(y + d, B), slot, i, d).wait_recv()
        return carry

    lax.fori_loop(0, N, kv_wait, 0)

    log2e = 1.4426950408889634
    factor = log2e / math.sqrt(HD)

    def a_copy(zz, src):
        return remote(att.at[zz], arr.at[src], as_.at[zz], ar.at[src], ulysses=zz)

    def attend(p, carry):
        zz = order(U - 1 - p)
        for h in range(H):
            qv = q[h, pl.ds(pl.multiple_of(zz * rows, rows), rows), :]

            def keys(b, state):
                high, den, num = state
                s = lax.dot_general(
                    qv, kv[b, 0, h], (((1,), (1,)), ((), ())), preferred_element_type=F32
                )
                lines = []
                for r in range(nbp):
                    qb = (zz * B + y) * nbp + r
                    lines.append(
                        jnp.concatenate(
                            [
                                bias_ref[h, qb, pl.ds((k // nbp * B + b) * nbp + k % nbp, 1), :]
                                for k in range(U * nbp)
                            ],
                            axis=1,
                        )
                    )
                s = jnp.concatenate(
                    [s[r * block:(r + 1) * block] * factor + lines[r] for r in range(nbp)], axis=0
                )
                new = jnp.maximum(high, jnp.max(s, axis=1, keepdims=True))
                wts = jnp.exp2(s - new)
                fix = jnp.exp2(high - new)
                den = den * fix + jnp.sum(wts, axis=1, keepdims=True)
                num = num * fix + jnp.dot(
                    wts.astype(BF16), kv[b, 1, h], preferred_element_type=F32
                )
                return new, den, num

            start = (
                jnp.full((rows, 1), -1e30, F32),
                jnp.zeros((rows, 1), F32),
                jnp.zeros((rows, HD), F32),
            )
            high, den, num = lax.fori_loop(0, B, keys, start)
            att[zz, :, h * HD:(h + 1) * HD] = (num / den).astype(BF16)

        @pl.when(p < U - 1)
        def _():
            a_copy(zz, z).start()

        return carry

    lax.fori_loop(0, U, attend, 0)
    arr[z] = att[z]
    for c in wo_copies:
        c.wait()
    for d in range(1, U):
        a_copy(lax.rem(z + d, U), lax.rem(z + d, U)).wait_recv()

    def product(col):
        acc = jnp.dot(arr[0], wo[col, 0], preferred_element_type=F32)
        for u in range(1, U):
            acc += jnp.dot(arr[u], wo[col, u], preferred_element_type=F32)
        return acc

    def p_copy(k):
        return remote(part.at[k], got.at[k], ps.at[k], pr.at[k], tensor=near)

    m_copy = remote(mid, far_got, ms, mr, tensor=far)
    part[0] = product(cross).astype(BF16)
    p_copy(0).start()
    there = product(far)
    p_copy(0).wait_recv()
    mid[...] = (there + got[0].astype(F32)).astype(BF16)
    m_copy.start()
    part[1] = product(near).astype(BF16)
    p_copy(1).start()
    here = product(t)
    p_copy(1).wait_recv()
    here = here + got[1].astype(F32)
    m_copy.wait_recv()
    out_ref[...] = (here + far_got[...].astype(F32)).astype(BF16)

    def drain(i, carry):
        zz, slot = piece_of(i)
        forward(i, lambda c: c.wait_send())
        x_copy(slot, t, i).wait_send()
        c_copy(slot, t, i).wait_send()
        f_copy(slot, far, i).wait_send()
        for d in range(1, B):
            kv_copy(y, slot, i, d).wait_send()
        return carry

    lax.fori_loop(0, N, drain, 0)
    for d in range(1, U):
        a_copy(lax.rem(z + d, U), z).wait_send()
    p_copy(0).wait_send()
    p_copy(1).wait_send()
    m_copy.wait_send()


def local(tokens, w_qkv, qkv_scale, block_mask, w_out):
    U, B, T = lax.axis_size("ulysses"), lax.axis_size("blk"), lax.axis_size("tensor")
    rows, feats = tokens.shape
    heads, blocks = block_mask.shape[0], block_mask.shape[1]
    cols = w_qkv.shape[2]
    hd = cols // heads
    block = U * B * rows // blocks
    ids = jnp.arange(blocks)
    allowed = (block_mask == 1) | (ids[:, None] == ids[None, :])[None]
    bias = jnp.broadcast_to(
        jnp.where(allowed, 0.0, -jnp.inf).astype(F32)[..., None], (heads, blocks, blocks, block)
    )
    R, N = rows // SUB, U * SUB
    dma = lambda *s: pltpu.SemaphoreType.DMA(s)
    vmem = pl.BlockSpec(memory_space=pltpu.VMEM)
    hbm = pl.BlockSpec(memory_space=pl.ANY)
    return pl.pallas_call(
        functools.partial(kernel, U, B, T),
        out_shape=jax.ShapeDtypeStruct((rows, feats), BF16),
        in_specs=[vmem, hbm, pl.BlockSpec(memory_space=pltpu.SMEM), vmem, hbm],
        out_specs=vmem,
        scratch_shapes=[
            pltpu.VMEM((N, T, R, feats), BF16),
            pltpu.VMEM((3, T * feats, cols), BF16),
            pltpu.VMEM((T, U, cols, feats), BF16),
            pltpu.VMEM((heads, U * rows, hd), BF16),
            pltpu.VMEM((B, 2, heads, U * rows, hd), BF16),
            pltpu.VMEM((U, rows, cols), BF16),
            pltpu.VMEM((U, rows, cols), BF16),
            pltpu.VMEM((2, rows, feats), BF16),
            pltpu.VMEM((2, rows, feats), BF16),
            pltpu.VMEM((rows, feats), BF16),
            pltpu.VMEM((rows, feats), BF16),
            pltpu.SemaphoreType.DMA,
            dma(T),
            dma(SUB),
            dma(N), dma(N), dma(SUB), dma(SUB),
            dma(N), dma(N), dma(N), dma(N), dma(N), dma(N),
            dma(B, N), dma(B, N),
            dma(U), dma(U),
            dma(2), dma(2),
            pltpu.SemaphoreType.DMA, pltpu.SemaphoreType.DMA,
        ],
        compiler_params=pltpu.CompilerParams(
            collective_id=0, has_side_effects=True, vmem_limit_bytes=62 * 1024 * 1024
        ),
    )(tokens, jnp.transpose(w_qkv, (1, 0, 2)), qkv_scale, bias, w_out)


def solution(mesh):
    return jax.shard_map(
        local,
        mesh=mesh,
        in_specs=(
            P(("ulysses", "blk"), "tensor"),
            P(None, None, ("ulysses", "tensor")),
            P(None, ("ulysses", "tensor")),
            P(("ulysses", "tensor"), None, None),
            P(None, "tensor", None),
        ),
        out_specs=P(("ulysses", "blk"), "tensor"),
        check_vma=False,
    )
```

time: 309 us -> 111 us (0.36)
  waiting for transfers between devices: 167 us -> 0 us
  Pallas kernels: 0 us -> 106 us
  matrix products: 66.7 us -> 0 us
  local copies, waits for them, and re-layouts: 27.4 us -> 4.1 us
  blocking collectives: 18.7 us -> 0 us
  other arithmetic: 14.2 us -> 0.73 us
  between operations: 13.2 us -> 0.01 us
    all_gather x3 -> x0, waiting for transfers between devices: 133 us -> none  [the longest x1 91.8 us: local(): lax.all_gather(tokens[None], ('ulysses', 'tensor'), axis=0, tiled=True)]
    pallas_call x0 -> x1, Pallas kernels: none -> 106 us  [local(): pl.pallas_call(functools.partial(kernel, U, B, T), out_shape=jax.ShapeDty...]
    dot_general x23 -> x0, matrix products: 66.6 us -> none  [the longest x16 41.7 us: one_shard(): jnp.einsum('rd,dcn->rcn', token_part, weights, preferred_element_type=jnp...]
    reduce_scatter x1 -> x0, waiting for transfers between devices: 32.7 us -> none  [local(): lax.psum_scatter(partial_value.astype(jnp.bfloat16), 'tensor', scatter_di...]
    dynamic_slice x18 -> x0, local copies, waits for them, and re-layouts: 19 us -> none  [the longest x16 15.1 us: one_shard(): current = lax.dynamic_index_in_dim(accum, group_id, 0, keepdims=False)]
    all_to_all x1 -> x0, blocking collectives: 18.7 us -> none  [local(): lax.all_to_all(grouped, 'ulysses', split_axis=1, concat_axis=0, tiled=True)]
    reduce_sum x2 -> x0, other arithmetic: 9.37 us -> none  [one_block(): denominator = denominator * factor + jnp.sum(weights, axis=-1)]
    convert_element_type x4 -> x0, other arithmetic: 3.39 us -> none  [the longest x1 3.03 us: local(): projected = projected.astype(jnp.bfloat16)]
  transfers between devices with their start and end apart: 4 -> 0, of which waited for: 4 -> 0; matrix products, arithmetic and copies ran while one was open for 0% -> 0% of each run, Pallas kernels for 0% -> 0%
where the time goes in v1:
time: 111 us
  Pallas kernels  106 us (95%)
  local copies, waits for them, and re-layouts  4.1 us (4%)
    pallas_call x1, Pallas kernels, local(): pl.pallas_call(functools.partial(kernel, U, B, T), out_shape=jax.ShapeDty...  106 us
    unnamed x2, local copies, waits for them, and re-layouts  3.27 us

profile of v1, /device:TPU:0, one launch (start us, length us, event | category | flops | bytes accessed | tf_op | source)
XLA Modules:
  0.0 111.1 jit_solution(5906468371874455648)
XLA Ops:
  0.0 1.3 %copy.6.scale_ref = f32[3,2]{1,0:T(4,128)} copy(f32[3,2]{0,1:T(2,128)} %param.7) | data formatting | bytes 48 | tf_op args[2]
  1.3 0.7 or_select_fusion
  2.0 0.8 broadcast_in_dim.19.bias_ref
  2.9 106.3 %shard_map.55 = bf16[256,1280]{1,0:T(8,128)(2,1)} custom-call(bf16[256,1280]{1,0:T(8,128)(2,1)} %x_ref.1, bf16[3,5120,256]{2,1,0:T(8,128)(2,1)} %bitcast.1, f32[3,2]{1,0:T(4,128)} %copy.6.scale_ref, f32[2,16,16,128]{3,2,1,0:T(8,128)} %broadcast_in_dim.19.bias_ref, bf16[4,256,5120]{2,1,0:T(8,128)(2,1)} %wo_hbm.1), custom_call_target="tpu_custom_call" | custom-call | tf_op jit(solution)/shard_map/pallas_call | solution.py:278
  109.2 2.0 %copy.8 = bf16[256,1280]{1,0:T(8,128)(2,1)} copy(bf16[256,1280]{1,0:T(8,128)(2,1)} %shard_map.55) | data formatting | bytes 1310720
  (1 shorter events, 0.0 us)

commit v2 on v1

--- a/solution.py
+++ b/solution.py
@@ -9,6 +9,7 @@
 from jax.sharding import PartitionSpec as P
 
 SUB = 2
+LAG = SUB + 1
 F32 = jnp.float32
 BF16 = jnp.bfloat16
 
@@ -16,7 +17,7 @@
 def kernel(U, B, T, x_ref, w_hbm, scale_ref, bias_ref, wo_hbm, out_ref,
            g, w, wo, q, kv, att, arr, part, got, mid, far_got,
            w_sem, wo_sem, own_sem,
-           zs, zr, up_s, dn_s, xs, xr, cs, cr, fs, fr, ks, kr, as_, ar, ps, pr, ms, mr):
+           zs, zr, up_s, dn_s, xs, xr, cs, cr, fs, fr, ks, kr, as_, ar, ps, pr, ms, mr, hs, hr):
     z, y, t = lax.axis_index("ulysses"), lax.axis_index("blk"), lax.axis_index("tensor")
     near = t + 1 - 2 * lax.rem(t, 2)
     far = lax.rem(t + T // 2, T)
@@ -51,10 +52,27 @@
     pl.semaphore_signal(barrier, inc=1, device_id={"tensor": far})
     pl.semaphore_wait(barrier, (U - 1) + (B - 1) + 2)
 
+    side = 1 - 2 * lax.rem(z, 2)
+    pair = z + side
+    skip_from = SUB + SUB // 2
+    skips = 2 * SUB - skip_from
+
+    def skipped(j):
+        return (j >= skip_from) & (j < skip_from + skips)
+
+    def landing(i):
+        late = jnp.where(i < N - skips, i + skips, i - (N - skips) + skip_from)
+        return jnp.where(i < skip_from, i, late)
+
+    def pair_copy(owner, j):
+        slot = owner * SUB + SUB // 2 + j
+        view = g.at[slot, far]
+        return remote(view, view, hs.at[j], hr.at[j], ulysses=pair)
+
     def order(p):
         m = jnp.minimum(z, U - 1 - z)
         half = (p + 1) // 2
-        near_z = jnp.where(lax.rem(p, 2) == 1, z - half, z + half)
+        near_z = jnp.where(lax.rem(p, 2) == 1, z + side * half, z - side * half)
         far_z = jnp.where(z < U - 1 - z, p, U - 1 - p)
         return jnp.where(p <= 2 * m, near_z, far_z)
 
@@ -112,14 +130,32 @@
                 z_copy(slot, zs.at[slot], lax.rem(z + 1, U)).wait_recv()
 
             forward(j, lambda c: c.start())
-            x_copy(slot, t, j).start()
+
+            @pl.when(jnp.logical_not(skipped(j)))
+            def _():
+                x_copy(slot, t, j).start()
+
             c_copy(slot, t, j).start()
 
-        @pl.when(j >= SUB)
-        def _():
-            i = j - SUB
+        @pl.when(j == N - 1)
+        def _():
+            for k in range(skips):
+                pair_copy(z, k).start()
+
+        @pl.when(j >= LAG)
+        def _():
+            i = landing(j - LAG)
             zz, slot = piece_of(i)
-            x_copy(slot, far, i).wait_recv()
+
+            @pl.when(jnp.logical_not(skipped(i)))
+            def _():
+                x_copy(slot, far, i).wait_recv()
+
+            for k in range(skips):
+                @pl.when(i == skip_from + k)
+                def _():
+                    pair_copy(pair, k).wait_recv()
+
             f_copy(slot, far, i).start()
             c_copy(slot, near, i).wait_recv()
 
@@ -146,7 +182,7 @@
 
         return carry
 
-    lax.fori_loop(0, N + SUB, step, 0)
+    lax.fori_loop(0, N + LAG, step, 0)
 
     def kv_wait(i, carry):
         zz, slot = piece_of(i)
@@ -244,7 +280,11 @@
     def drain(i, carry):
         zz, slot = piece_of(i)
         forward(i, lambda c: c.wait_send())
-        x_copy(slot, t, i).wait_send()
+
+        @pl.when(jnp.logical_not(skipped(i)))
+        def _():
+            x_copy(slot, t, i).wait_send()
+
         c_copy(slot, t, i).wait_send()
         f_copy(slot, far, i).wait_send()
         for d in range(1, B):
@@ -252,6 +292,8 @@
         return carry
 
     lax.fori_loop(0, N, drain, 0)
+    for k in range(skips):
+        pair_copy(z, k).wait_send()
     for d in range(1, U):
         a_copy(lax.rem(z + d, U), z).wait_send()
     p_copy(0).wait_send()
@@ -301,6 +343,7 @@
             dma(U), dma(U),
             dma(2), dma(2),
             pltpu.SemaphoreType.DMA, pltpu.SemaphoreType.DMA,
+            dma(SUB), dma(SUB),
         ],
         compiler_params=pltpu.CompilerParams(
             collective_id=0, has_side_effects=True, vmem_limit_bytes=62 * 1024 * 1024

time: 111 us -> 112 us (level)
  no operation moved by 1% of the time
where the time goes in v2:
time: 112 us
  Pallas kernels  107 us (96%)
  local copies, waits for them, and re-layouts  4.1 us (4%)
    pallas_call x1, Pallas kernels, local(): pl.pallas_call(functools.partial(kernel, U, B, T), out_shape=jax.ShapeDty...  107 us
    unnamed x2, local copies, waits for them, and re-layouts  3.27 us

profile of v2, /device:TPU:0, one launch (start us, length us, event | category | flops | bytes accessed | tf_op | source)
XLA Modules:
  0.0 111.7 jit_solution(16275329525665734704)
XLA Ops:
  0.0 1.3 %copy.6.scale_ref = f32[3,2]{1,0:T(4,128)} copy(f32[3,2]{0,1:T(2,128)} %param.7) | data formatting | bytes 48 | tf_op args[2]
  1.3 0.7 or_select_fusion
  2.0 0.8 broadcast_in_dim.19.bias_ref
  2.9 106.9 %shard_map.55 = bf16[256,1280]{1,0:T(8,128)(2,1)} custom-call(bf16[256,1280]{1,0:T(8,128)(2,1)} %x_ref.1, bf16[3,5120,256]{2,1,0:T(8,128)(2,1)} %bitcast.1, f32[3,2]{1,0:T(4,128)} %copy.6.scale_ref, f32[2,16,16,128]{3,2,1,0:T(8,128)} %broadcast_in_dim.19.bias_ref, bf16[4,256,5120]{2,1,0:T(8,128)(2,1)} %wo_hbm.1), custom_call_target="tpu_custom_call" | custom-call | tf_op jit(solution)/shard_map/pallas_call | solution.py:320
  109.7 2.0 %copy.8 = bf16[256,1280]{1,0:T(8,128)(2,1)} copy(bf16[256,1280]{1,0:T(8,128)(2,1)} %shard_map.55) | data formatting | bytes 1310720
  (1 shorter events, 0.0 us)

commit v3 on v2

--- a/solution.py
+++ b/solution.py
@@ -9,7 +9,8 @@
 from jax.sharding import PartitionSpec as P
 
 SUB = 2
-LAG = SUB + 1
+LAG = 2 * SUB
+HALVES = 2
 F32 = jnp.float32
 BF16 = jnp.bfloat16
 
@@ -29,19 +30,16 @@
     nbp = rows // bias_ref.shape[3]
     block = bias_ref.shape[3]
 
+    def own_copy(s):
+        return pltpu.make_async_copy(x_ref.at[pl.ds(s * R, R)], g.at[z * SUB + s, t], own_sem.at[s])
+
+    for s in range(SUB):
+        own_copy(s).start()
     w_copy = pltpu.make_async_copy(w_hbm, w, w_sem)
-    w_copy.start()
     wo_copies = [
         pltpu.make_async_copy(wo_hbm.at[:, :, pl.ds(j * feats, feats)], wo.at[j], wo_sem.at[j])
         for j in range(T)
     ]
-    for c in wo_copies:
-        c.start()
-    for s in range(SUB):
-        c = pltpu.make_async_copy(x_ref.at[pl.ds(s * R, R)], g.at[z * SUB + s, t], own_sem.at[s])
-        c.start()
-    for s in range(SUB):
-        pltpu.make_async_copy(x_ref.at[pl.ds(s * R, R)], g.at[z * SUB + s, t], own_sem.at[s]).wait()
 
     barrier = pltpu.get_barrier_semaphore()
     for d in range(1, U):
@@ -69,6 +67,9 @@
         view = g.at[slot, far]
         return remote(view, view, hs.at[j], hr.at[j], ulysses=pair)
 
+    for s in range(SUB):
+        own_copy(s).wait()
+
     def order(p):
         m = jnp.minimum(z, U - 1 - z)
         half = (p + 1) // 2
@@ -136,6 +137,15 @@
                 x_copy(slot, t, j).start()
 
             c_copy(slot, t, j).start()
+
+        @pl.when(j == SUB - 1)
+        def _():
+            w_copy.start()
+
+        @pl.when(j == 2 * SUB)
+        def _():
+            for c in wo_copies:
+                c.start()
 
         @pl.when(j == N - 1)
         def _():
@@ -195,13 +205,19 @@
     log2e = 1.4426950408889634
     factor = log2e / math.sqrt(HD)
 
-    def a_copy(zz, src):
-        return remote(att.at[zz], arr.at[src], as_.at[zz], ar.at[src], ulysses=zz)
-
-    def attend(p, carry):
+    HR = rows // HALVES
+    nbh = nbp // HALVES
+
+    def a_copy(hf, zz, src):
+        return remote(
+            att.at[hf, zz], arr.at[hf, src], as_.at[hf, zz], ar.at[hf, src], ulysses=zz
+        )
+
+    def attend(turn, carry):
+        hf, p = turn // U, lax.rem(turn, U)
         zz = order(U - 1 - p)
         for h in range(H):
-            qv = q[h, pl.ds(pl.multiple_of(zz * rows, rows), rows), :]
+            qv = q[h, pl.ds(pl.multiple_of(zz * rows + hf * HR, HR), HR), :]
 
             def keys(b, state):
                 high, den, num = state
@@ -209,8 +225,8 @@
                     qv, kv[b, 0, h], (((1,), (1,)), ((), ())), preferred_element_type=F32
                 )
                 lines = []
-                for r in range(nbp):
-                    qb = (zz * B + y) * nbp + r
+                for r in range(nbh):
+                    qb = (zz * B + y) * nbp + hf * nbh + r
                     lines.append(
                         jnp.concatenate(
                             [
@@ -221,7 +237,7 @@
                         )
                     )
                 s = jnp.concatenate(
-                    [s[r * block:(r + 1) * block] * factor + lines[r] for r in range(nbp)], axis=0
+                    [s[r * block:(r + 1) * block] * factor + lines[r] for r in range(nbh)], axis=0
                 )
                 new = jnp.maximum(high, jnp.max(s, axis=1, keepdims=True))
                 wts = jnp.exp2(s - new)
@@ -233,49 +249,53 @@
                 return new, den, num
 
             start = (
-                jnp.full((rows, 1), -1e30, F32),
-                jnp.zeros((rows, 1), F32),
-                jnp.zeros((rows, HD), F32),
+                jnp.full((HR, 1), -1e30, F32),
+                jnp.zeros((HR, 1), F32),
+                jnp.zeros((HR, HD), F32),
             )
             high, den, num = lax.fori_loop(0, B, keys, start)
-            att[zz, :, h * HD:(h + 1) * HD] = (num / den).astype(BF16)
+            att[hf, zz, :, h * HD:(h + 1) * HD] = (num / den).astype(BF16)
 
         @pl.when(p < U - 1)
         def _():
-            a_copy(zz, z).start()
+            a_copy(hf, zz, z).start()
 
         return carry
 
-    lax.fori_loop(0, U, attend, 0)
-    arr[z] = att[z]
+    lax.fori_loop(0, U * HALVES, attend, 0)
     for c in wo_copies:
         c.wait()
-    for d in range(1, U):
-        a_copy(lax.rem(z + d, U), lax.rem(z + d, U)).wait_recv()
-
-    def product(col):
-        acc = jnp.dot(arr[0], wo[col, 0], preferred_element_type=F32)
+
+    def product(hf, col):
+        acc = jnp.dot(arr[hf, 0], wo[col, 0], preferred_element_type=F32)
         for u in range(1, U):
-            acc += jnp.dot(arr[u], wo[col, u], preferred_element_type=F32)
+            acc += jnp.dot(arr[hf, u], wo[col, u], preferred_element_type=F32)
         return acc
 
-    def p_copy(k):
-        return remote(part.at[k], got.at[k], ps.at[k], pr.at[k], tensor=near)
-
-    m_copy = remote(mid, far_got, ms, mr, tensor=far)
-    part[0] = product(cross).astype(BF16)
-    p_copy(0).start()
-    there = product(far)
-    p_copy(0).wait_recv()
-    mid[...] = (there + got[0].astype(F32)).astype(BF16)
-    m_copy.start()
-    part[1] = product(near).astype(BF16)
-    p_copy(1).start()
-    here = product(t)
-    p_copy(1).wait_recv()
-    here = here + got[1].astype(F32)
-    m_copy.wait_recv()
-    out_ref[...] = (here + far_got[...].astype(F32)).astype(BF16)
+    def p_copy(hf, k):
+        return remote(part.at[hf, k], got.at[hf, k], ps.at[hf, k], pr.at[hf, k], tensor=near)
+
+    def m_copy(hf):
+        return remote(mid.at[hf], far_got.at[hf], ms.at[hf], mr.at[hf], tensor=far)
+
+    for hf in range(HALVES):
+        arr[hf, z] = att[hf, z]
+        for d in range(1, U):
+            a_copy(hf, lax.rem(z + d, U), lax.rem(z + d, U)).wait_recv()
+        part[hf, 0] = product(hf, cross).astype(BF16)
+        p_copy(hf, 0).start()
+        there = product(hf, far)
+        p_copy(hf, 0).wait_recv()
+        mid[hf] = (there + got[hf, 0].astype(F32)).astype(BF16)
+        m_copy(hf).start()
+        part[hf, 1] = product(hf, near).astype(BF16)
+        p_copy(hf, 1).start()
+    for hf in range(HALVES):
+        here = product(hf, t)
+        p_copy(hf, 1).wait_recv()
+        here = here + got[hf, 1].astype(F32)
+        m_copy(hf).wait_recv()
+        out_ref[hf * HR:(hf + 1) * HR, :] = (here + far_got[hf].astype(F32)).astype(BF16)
 
     def drain(i, carry):
         zz, slot = piece_of(i)
@@ -294,11 +314,12 @@
     lax.fori_loop(0, N, drain, 0)
     for k in range(skips):
         pair_copy(z, k).wait_send()
-    for d in range(1, U):
-        a_copy(lax.rem(z + d, U), z).wait_send()
-    p_copy(0).wait_send()
-    p_copy(1).wait_send()
-    m_copy.wait_send()
+    for hf in range(HALVES):
+        for d in range(1, U):
+            a_copy(hf, lax.rem(z + d, U), z).wait_send()
+        p_copy(hf, 0).wait_send()
+        p_copy(hf, 1).wait_send()
+        m_copy(hf).wait_send()
 
 
 def local(tokens, w_qkv, qkv_scale, block_mask, w_out):
@@ -328,21 +349,21 @@
             pltpu.VMEM((T, U, cols, feats), BF16),
             pltpu.VMEM((heads, U * rows, hd), BF16),
             pltpu.VMEM((B, 2, heads, U * rows, hd), BF16),
-            pltpu.VMEM((U, rows, cols), BF16),
-            pltpu.VMEM((U, rows, cols), BF16),
-            pltpu.VMEM((2, rows, feats), BF16),
-            pltpu.VMEM((2, rows, feats), BF16),
-            pltpu.VMEM((rows, feats), BF16),
-            pltpu.VMEM((rows, feats), BF16),
+            pltpu.VMEM((HALVES, U, rows // HALVES, cols), BF16),
+            pltpu.VMEM((HALVES, U, rows // HALVES, cols), BF16),
+            pltpu.VMEM((HALVES, 2, rows // HALVES, feats), BF16),
+            pltpu.VMEM((HALVES, 2, rows // HALVES, feats), BF16),
+            pltpu.VMEM((HALVES, rows // HALVES, feats), BF16),
+            pltpu.VMEM((HALVES, rows // HALVES, feats), BF16),
             pltpu.SemaphoreType.DMA,
             dma(T),
             dma(SUB),
             dma(N), dma(N), dma(SUB), dma(SUB),
             dma(N), dma(N), dma(N), dma(N), dma(N), dma(N),
             dma(B, N), dma(B, N),
-            dma(U), dma(U),
-            dma(2), dma(2),
-            pltpu.SemaphoreType.DMA, pltpu.SemaphoreType.DMA,
+            dma(HALVES, U), dma(HALVES, U),
+            dma(HALVES, 2), dma(HALVES, 2),
+            dma(HALVES), dma(HALVES),
             dma(SUB), dma(SUB),
         ],
         compiler_params=pltpu.CompilerParams(

time: 112 us -> 114 us (1.018)
  Pallas kernels: 107 us -> 109 us
    pallas_call x1, Pallas kernels: 107 us -> 109 us  [local(): pl.pallas_call(functools.partial(kernel, U, B, T), out_shape=jax.ShapeDty...]
where the time goes in v3:
time: 114 us
  Pallas kernels  109 us (96%)
  local copies, waits for them, and re-layouts  4.1 us (4%)
    pallas_call x1, Pallas kernels, local(): pl.pallas_call(functools.partial(kernel, U, B, T), out_shape=jax.ShapeDty...  109 us
    unnamed x2, local copies, waits for them, and re-layouts  3.27 us

profile of v3, /device:TPU:0, one launch (start us, length us, event | category | flops | bytes accessed | tf_op | source)
XLA Modules:
  0.0 114.0 jit_solution(2999678808031124628)
XLA Ops:
  0.0 1.3 %copy.6.scale_ref = f32[3,2]{1,0:T(4,128)} copy(f32[3,2]{0,1:T(2,128)} %param.7) | data formatting | bytes 48 | tf_op args[2]
  1.3 0.7 or_select_fusion
  2.0 0.8 broadcast_in_dim.19.bias_ref
  2.9 109.1 %shard_map.55 = bf16[256,1280]{1,0:T(8,128)(2,1)} custom-call(bf16[256,1280]{1,0:T(8,128)(2,1)} %x_ref.1, bf16[3,5120,256]{2,1,0:T(8,128)(2,1)} %bitcast.1, f32[3,2]{1,0:T(4,128)} %copy.6.scale_ref, f32[2,16,16,128]{3,2,1,0:T(8,128)} %broadcast_in_dim.19.bias_ref, bf16[4,256,5120]{2,1,0:T(8,128)(2,1)} %wo_hbm.1), custom_call_target="tpu_custom_call" | custom-call | tf_op jit(solution)/shard_map/pallas_call | solution.py:341
  112.0 2.0 %copy.8 = bf16[256,1280]{1,0:T(8,128)(2,1)} copy(bf16[256,1280]{1,0:T(8,128)(2,1)} %shard_map.55) | data formatting | bytes 1310720
  (1 shorter events, 0.0 us)
